TPU v7x, 128 devices: a whole 4x4x4 slice. The times are simulated.
128 devices in a mesh: grp: 4 (over z), wide: 32 (over y, x, core).
Axes of the slice: x: 4, y: 4, z: 4, core: 2. Of those that a mesh axis runs over, the one named last changes fastest.
Arguments:
- visibilities: bfloat16 [2, 8, 2048, 4096], P(None, None, 'wide', 'grp'), may hold values from -6 to 6
- filters: bfloat16 [4096, 64, 2048], P(('grp', 'wide')), may hold values from -0.125 to 0.125
- counts: int32 [4096], replicated, may hold values from 128 to 2048, as said below
- m_of_slot: int32 [4096], replicated, may hold values from 0 to 4095, each once
- band_of_block: int32 [4096, 8], replicated, may hold values from 0 to 1023
Outputs:
- kl_coeffs: bfloat16 [4096, 2, 8, 64], P(('grp', 'wide'))
- band_power: float32 [8, 1024], P(None, ('grp', 'wide'))
Inputs may be any that keep to these rules, and one draw needn't show every extreme that they name: Mode m uses its first counts[m] baselines; both ends of the range are taken in every draw. `m_of_slot`: each m mode stands in exactly one slot.
All inputs are finite; a program needn't handle non-finite values.
Results may differ from a plain program's by a relative error of at most 0.0055.
Values may be sent and summed in bfloat16 or wider, within the bound.
No kernel may reach another device: no remote copies, remote signals or barrier semaphores. Data moves between devices by JAX's collectives and lax.ppermute only.
A program may use at most 128 MiB of HBM per device.

v0:
```python
import math

import jax
import jax.numpy as jnp
from jax import lax
from jax.sharding import PartitionSpec as P

NB = 2048
NT = 4096
KL = 64
KB = 8
NBAND = 1024
NKB = 8


def table_block(columns):
    times = jnp.arange(NT, dtype=jnp.int32)
    index = times[:, None] * columns[None, :] % NT
    angles = index.astype(jnp.float32) * (2.0 * math.pi / NT)
    return (jnp.cos(angles).astype(jnp.bfloat16), jnp.sin(angles).astype(jnp.bfloat16))


def body(visibilities, filters, counts, m_of_slot, band_of_block):
    highest = lax.Precision.HIGHEST
    channels = visibilities.shape[1]
    local = lax.all_to_all(visibilities, "grp", split_axis=2, concat_axis=3, tiled=True)
    base_dev = local.shape[2]
    rows = channels * base_dev
    real_part = local[0].reshape(rows, NT)
    imag_part = local[1].reshape(rows, NT)
    scale_dft = 1.0 / math.sqrt(NT)
    mode_block = min(512, NT)

    def product(table, values):
        return jnp.einsum("tm,rt->mr", table, values, preferred_element_type=jnp.float32)

    def transform(columns):
        cos_table, sin_table = table_block(columns)
        spec_re = (product(cos_table, real_part) + product(sin_table, imag_part)) * scale_dft
        spec_im = (product(cos_table, imag_part) - product(sin_table, real_part)) * scale_dft
        return jnp.stack([spec_re, spec_im]).astype(jnp.bfloat16)

    blocks = lax.map(transform, m_of_slot.reshape(NT // mode_block, mode_block))
    spectrum = blocks.transpose(1, 0, 2, 3).reshape(2, NT, rows)
    groups = lax.axis_size("grp")
    wides = lax.axis_size("wide")
    slots = NT // (groups * wides)
    moved = lax.all_to_all(spectrum, ("grp", "wide"), split_axis=1, concat_axis=2, tiled=True)
    owned = moved.reshape(2, slots, groups, wides, channels, base_dev).transpose(1, 0, 4, 3, 2, 5)
    owned = owned.reshape(slots, 2, channels, NB)
    place = lax.axis_index(("grp", "wide"))
    mine = lax.dynamic_slice_in_dim(m_of_slot, place * slots, slots)
    active_counts = counts[mine]
    band_rows = band_of_block[mine]
    active = jnp.arange(NB, dtype=jnp.int32)[None, :] < active_counts[:, None]
    masked = jnp.where(active[:, None, None, :], owned, jnp.zeros_like(owned))
    coeffs = jnp.einsum("sxcb,skb->sxck", masked, filters, preferred_element_type=jnp.float32)
    kl_coeffs = coeffs.astype(jnp.bfloat16)
    power = coeffs[:, 0] * coeffs[:, 0] + coeffs[:, 1] * coeffs[:, 1]
    block_power = power.reshape(slots, channels, NKB, KB).sum(axis=-1)
    one_hot = (band_rows[:, :, None] == jnp.arange(NBAND, dtype=jnp.int32)[None, None, :]).astype(
        jnp.float32
    )
    partial_sums = jnp.einsum("scj,sjn->cn", block_power, one_hot, precision=highest)
    band_scale = NBAND / (NT * KL)
    band_power = (
        lax.psum_scatter(partial_sums, ("grp", "wide"), scatter_dimension=1, tiled=True)
        * band_scale
    )
    return (kl_coeffs, band_power)


def solution(mesh):
    placed = (P(None, None, "wide", "grp"), P(("grp", "wide"), None, None), P(), P(), P())
    return jax.shard_map(
        body,
        mesh=mesh,
        in_specs=placed,
        out_specs=(P(("grp", "wide"), None, None, None), P(None, ("grp", "wide"))),
        check_vma=False,
    )
```

profile of v0, /device:TPU:1, one launch (start us, length us, event | category | flops | bytes accessed | tf_op | source)
XLA Modules:
  0.0 1225.0 jit_solution(2172473711864143579)
XLA Ops:
  0.6 0.0 copy-start
  0.6 0.0 copy-start.5
  0.7 4.1 copy.18
  4.7 5.8 all-to-all-start
  10.6 25.5 %all-to-all-done = bf16[2,8,64,1024]{3,1,0,2:T(8,128)(2,1)S(1)} async-done(((bf16[2,8,64,1024]{3,1,0,2:T(8,128)(2,1)}), bf16[2,8,64,1024]{3,1,0,2:T(8,128)(2,1)S(1)}, u32[]{:S(2)}, u32[]{:S(2)}) %all-to-all-start) | async-done | bytes 2097184 | tf_op jit(solution)/shard_map/all_to_all | solution.py:26
  36.0 0.2 fusion.40
  36.2 0.8 copy.19
  37.0 0.4 copy.35
  37.4 0.8 copy.20
  38.2 1.4 copy.36
  39.6 1008.2 %while.12 = (s32[]{:T(128)}, bf16[8,2,512,128]{3,2,0,1:T(8,128)(2,1)S(1)}, s32[8,512]{1,0:T(8,128)S(1)}, bf16[128,4096]{1,0:T(8,128)(2,1)S(1)}, bf16[128,4096]{1,0:T(8,128)(2,1)}, /*index=5*/s32[]{:T(128)}) while((s32[]{:T(128)}, bf16[8,2,512,128]{3,2,0,1:T(8,128)(2,1)S(1)}, s32[8,512]{1,0:T(8,128)S(1)}, bf16[128,4096]{1,0:T(8,128)(2,1)S(1)}, ...), condition=%wide.region_1.2_spmd, body=%wide.region_0.1_spmd.sunk | while | flops 2274230272 | bytes 10236009 | solution.py:43
  40.1 30.8 %fusion.62 = f32[512,128]{1,0:T(8,128)S(1)} fusion(bf16[128,4096]{1,0:T(8,128)(2,1)S(1)} %get-tuple-element.129, s32[512]{0:T(512)S(1)} %bitcast.73), kind=kOutput, calls=%fused_computation.14.clone.1 | convolution fusion | flops 568328192 | bytes 1312768 | tf_op jit(solution)/shard_map/while/body/eval_jaxpr/tm,rt->mr/dot_general | solution.py:35
  71.0 31.9 %fusion.63 = bf16[1,1,512,128]{3,2,1,0:T(8,128)(2,1)S(1)} fusion(f32[512,128]{1,0:T(8,128)S(1)} %fusion.62, bf16[128,4096]{1,0:T(8,128)(2,1)S(1)} %copy-done.3, s32[512]{0:T(512)S(1)} %bitcast.74), kind=kOutput, calls=%fused_computation.23.clone.1 | convolution fusion | flops 568524800 | bytes 1443840 | tf_op jit(solution)/shard_map/while/body/eval_jaxpr/tm,rt->mr/dot_general | solution.py:35
  102.9 30.8 %fusion.60 = f32[512,128]{1,0:T(8,128)S(1)} fusion(bf16[128,4096]{1,0:T(8,128)(2,1)S(1)} %copy-done.3, s32[512]{0:T(512)S(1)} %bitcast.75), kind=kOutput, calls=%fused_computation.13.clone.1 | convolution fusion | flops 568328192 | bytes 1312768 | tf_op jit(solution)/shard_map/while/body/eval_jaxpr/tm,rt->mr/dot_general | solution.py:35
  133.8 31.3 %fusion.61 = bf16[1,1,512,128]{3,2,1,0:T(8,128)(2,1)S(1)} fusion(f32[512,128]{1,0:T(8,128)S(1)} %fusion.60, bf16[128,4096]{1,0:T(8,128)(2,1)S(1)} %get-tuple-element.129, s32[512]{0:T(512)S(1)} %bitcast.76), kind=kOutput, calls=%fused_computation.24.clone.1 | convolution fusion | flops 568524800 | bytes 1443840 | tf_op jit(solution)/shard_map/while/body/eval_jaxpr/tm,rt->mr/dot_general | solution.py:35
  165.6 30.8 %fusion.62 = f32[512,128]{1,0:T(8,128)S(1)} fusion(bf16[128,4096]{1,0:T(8,128)(2,1)S(1)} %get-tuple-element.129, s32[512]{0:T(512)S(1)} %bitcast.73), kind=kOutput, calls=%fused_computation.14.clone.1 | convolution fusion | flops 568328192 | bytes 1312768 | tf_op jit(solution)/shard_map/while/body/eval_jaxpr/tm,rt->mr/dot_general | solution.py:35
  196.4 31.9 %fusion.63 = bf16[1,1,512,128]{3,2,1,0:T(8,128)(2,1)S(1)} fusion(f32[512,128]{1,0:T(8,128)S(1)} %fusion.62, bf16[128,4096]{1,0:T(8,128)(2,1)S(1)} %copy-done.3, s32[512]{0:T(512)S(1)} %bitcast.74), kind=kOutput, calls=%fused_computation.23.clone.1 | convolution fusion | flops 568524800 | bytes 1443840 | tf_op jit(solution)/shard_map/while/body/eval_jaxpr/tm,rt->mr/dot_general | solution.py:35
  228.4 30.8 %fusion.60 = f32[512,128]{1,0:T(8,128)S(1)} fusion(bf16[128,4096]{1,0:T(8,128)(2,1)S(1)} %copy-done.3, s32[512]{0:T(512)S(1)} %bitcast.75), kind=kOutput, calls=%fused_computation.13.clone.1 | convolution fusion | flops 568328192 | bytes 1312768 | tf_op jit(solution)/shard_map/while/body/eval_jaxpr/tm,rt->mr/dot_general | solution.py:35
  259.2 31.3 %fusion.61 = bf16[1,1,512,128]{3,2,1,0:T(8,128)(2,1)S(1)} fusion(f32[512,128]{1,0:T(8,128)S(1)} %fusion.60, bf16[128,4096]{1,0:T(8,128)(2,1)S(1)} %get-tuple-element.129, s32[512]{0:T(512)S(1)} %bitcast.76), kind=kOutput, calls=%fused_computation.24.clone.1 | convolution fusion | flops 568524800 | bytes 1443840 | tf_op jit(solution)/shard_map/while/body/eval_jaxpr/tm,rt->mr/dot_general | solution.py:35
  291.0 30.8 %fusion.62 = f32[512,128]{1,0:T(8,128)S(1)} fusion(bf16[128,4096]{1,0:T(8,128)(2,1)S(1)} %get-tuple-element.129, s32[512]{0:T(512)S(1)} %bitcast.73), kind=kOutput, calls=%fused_computation.14.clone.1 | convolution fusion | flops 568328192 | bytes 1312768 | tf_op jit(solution)/shard_map/while/body/eval_jaxpr/tm,rt->mr/dot_general | solution.py:35
  321.9 31.9 %fusion.63 = bf16[1,1,512,128]{3,2,1,0:T(8,128)(2,1)S(1)} fusion(f32[512,128]{1,0:T(8,128)S(1)} %fusion.62, bf16[128,4096]{1,0:T(8,128)(2,1)S(1)} %copy-done.3, s32[512]{0:T(512)S(1)} %bitcast.74), kind=kOutput, calls=%fused_computation.23.clone.1 | convolution fusion | flops 568524800 | bytes 1443840 | tf_op jit(solution)/shard_map/while/body/eval_jaxpr/tm,rt->mr/dot_general | solution.py:35
  353.8 30.8 %fusion.60 = f32[512,128]{1,0:T(8,128)S(1)} fusion(bf16[128,4096]{1,0:T(8,128)(2,1)S(1)} %copy-done.3, s32[512]{0:T(512)S(1)} %bitcast.75), kind=kOutput, calls=%fused_computation.13.clone.1 | convolution fusion | flops 568328192 | bytes 1312768 | tf_op jit(solution)/shard_map/while/body/eval_jaxpr/tm,rt->mr/dot_general | solution.py:35
  384.7 31.3 %fusion.61 = bf16[1,1,512,128]{3,2,1,0:T(8,128)(2,1)S(1)} fusion(f32[512,128]{1,0:T(8,128)S(1)} %fusion.60, bf16[128,4096]{1,0:T(8,128)(2,1)S(1)} %get-tuple-element.129, s32[512]{0:T(512)S(1)} %bitcast.76), kind=kOutput, calls=%fused_computation.24.clone.1 | convolution fusion | flops 568524800 | bytes 1443840 | tf_op jit(solution)/shard_map/while/body/eval_jaxpr/tm,rt->mr/dot_general | solution.py:35
  416.5 30.8 %fusion.62 = f32[512,128]{1,0:T(8,128)S(1)} fusion(bf16[128,4096]{1,0:T(8,128)(2,1)S(1)} %get-tuple-element.129, s32[512]{0:T(512)S(1)} %bitcast.73), kind=kOutput, calls=%fused_computation.14.clone.1 | convolution fusion | flops 568328192 | bytes 1312768 | tf_op jit(solution)/shard_map/while/body/eval_jaxpr/tm,rt->mr/dot_general | solution.py:35
  447.3 31.9 %fusion.63 = bf16[1,1,512,128]{3,2,1,0:T(8,128)(2,1)S(1)} fusion(f32[512,128]{1,0:T(8,128)S(1)} %fusion.62, bf16[128,4096]{1,0:T(8,128)(2,1)S(1)} %copy-done.3, s32[512]{0:T(512)S(1)} %bitcast.74), kind=kOutput, calls=%fused_computation.23.clone.1 | convolution fusion | flops 568524800 | bytes 1443840 | tf_op jit(solution)/shard_map/while/body/eval_jaxpr/tm,rt->mr/dot_general | solution.py:35
  479.3 30.8 %fusion.60 = f32[512,128]{1,0:T(8,128)S(1)} fusion(bf16[128,4096]{1,0:T(8,128)(2,1)S(1)} %copy-done.3, s32[512]{0:T(512)S(1)} %bitcast.75), kind=kOutput, calls=%fused_computation.13.clone.1 | convolution fusion | flops 568328192 | bytes 1312768 | tf_op jit(solution)/shard_map/while/body/eval_jaxpr/tm,rt->mr/dot_general | solution.py:35
  510.1 31.3 %fusion.61 = bf16[1,1,512,128]{3,2,1,0:T(8,128)(2,1)S(1)} fusion(f32[512,128]{1,0:T(8,128)S(1)} %fusion.60, bf16[128,4096]{1,0:T(8,128)(2,1)S(1)} %get-tuple-element.129, s32[512]{0:T(512)S(1)} %bitcast.76), kind=kOutput, calls=%fused_computation.24.clone.1 | convolution fusion | flops 568524800 | bytes 1443840 | tf_op jit(solution)/shard_map/while/body/eval_jaxpr/tm,rt->mr/dot_general | solution.py:35
  541.9 30.8 %fusion.62 = f32[512,128]{1,0:T(8,128)S(1)} fusion(bf16[128,4096]{1,0:T(8,128)(2,1)S(1)} %get-tuple-element.129, s32[512]{0:T(512)S(1)} %bitcast.73), kind=kOutput, calls=%fused_computation.14.clone.1 | convolution fusion | flops 568328192 | bytes 1312768 | tf_op jit(solution)/shard_map/while/body/eval_jaxpr/tm,rt->mr/dot_general | solution.py:35
  572.8 31.9 %fusion.63 = bf16[1,1,512,128]{3,2,1,0:T(8,128)(2,1)S(1)} fusion(f32[512,128]{1,0:T(8,128)S(1)} %fusion.62, bf16[128,4096]{1,0:T(8,128)(2,1)S(1)} %copy-done.3, s32[512]{0:T(512)S(1)} %bitcast.74), kind=kOutput, calls=%fused_computation.23.clone.1 | convolution fusion | flops 568524800 | bytes 1443840 | tf_op jit(solution)/shard_map/while/body/eval_jaxpr/tm,rt->mr/dot_general | solution.py:35
  604.7 30.8 %fusion.60 = f32[512,128]{1,0:T(8,128)S(1)} fusion(bf16[128,4096]{1,0:T(8,128)(2,1)S(1)} %copy-done.3, s32[512]{0:T(512)S(1)} %bitcast.75), kind=kOutput, calls=%fused_computation.13.clone.1 | convolution fusion | flops 568328192 | bytes 1312768 | tf_op jit(solution)/shard_map/while/body/eval_jaxpr/tm,rt->mr/dot_general | solution.py:35
  635.6 31.3 %fusion.61 = bf16[1,1,512,128]{3,2,1,0:T(8,128)(2,1)S(1)} fusion(f32[512,128]{1,0:T(8,128)S(1)} %fusion.60, bf16[128,4096]{1,0:T(8,128)(2,1)S(1)} %get-tuple-element.129, s32[512]{0:T(512)S(1)} %bitcast.76), kind=kOutput, calls=%fused_computation.24.clone.1 | convolution fusion | flops 568524800 | bytes 1443840 | tf_op jit(solution)/shard_map/while/body/eval_jaxpr/tm,rt->mr/dot_general | solution.py:35
  667.4 30.8 %fusion.62 = f32[512,128]{1,0:T(8,128)S(1)} fusion(bf16[128,4096]{1,0:T(8,128)(2,1)S(1)} %get-tuple-element.129, s32[512]{0:T(512)S(1)} %bitcast.73), kind=kOutput, calls=%fused_computation.14.clone.1 | convolution fusion | flops 568328192 | bytes 1312768 | tf_op jit(solution)/shard_map/while/body/eval_jaxpr/tm,rt->mr/dot_general | solution.py:35
  698.3 31.9 %fusion.63 = bf16[1,1,512,128]{3,2,1,0:T(8,128)(2,1)S(1)} fusion(f32[512,128]{1,0:T(8,128)S(1)} %fusion.62, bf16[128,4096]{1,0:T(8,128)(2,1)S(1)} %copy-done.3, s32[512]{0:T(512)S(1)} %bitcast.74), kind=kOutput, calls=%fused_computation.23.clone.1 | convolution fusion | flops 568524800 | bytes 1443840 | tf_op jit(solution)/shard_map/while/body/eval_jaxpr/tm,rt->mr/dot_general | solution.py:35
  730.2 30.8 %fusion.60 = f32[512,128]{1,0:T(8,128)S(1)} fusion(bf16[128,4096]{1,0:T(8,128)(2,1)S(1)} %copy-done.3, s32[512]{0:T(512)S(1)} %bitcast.75), kind=kOutput, calls=%fused_computation.13.clone.1 | convolution fusion | flops 568328192 | bytes 1312768 | tf_op jit(solution)/shard_map/while/body/eval_jaxpr/tm,rt->mr/dot_general | solution.py:35
  761.0 31.3 %fusion.61 = bf16[1,1,512,128]{3,2,1,0:T(8,128)(2,1)S(1)} fusion(f32[512,128]{1,0:T(8,128)S(1)} %fusion.60, bf16[128,4096]{1,0:T(8,128)(2,1)S(1)} %get-tuple-element.129, s32[512]{0:T(512)S(1)} %bitcast.76), kind=kOutput, calls=%fused_computation.24.clone.1 | convolution fusion | flops 568524800 | bytes 1443840 | tf_op jit(solution)/shard_map/while/body/eval_jaxpr/tm,rt->mr/dot_general | solution.py:35
  792.9 30.8 %fusion.62 = f32[512,128]{1,0:T(8,128)S(1)} fusion(bf16[128,4096]{1,0:T(8,128)(2,1)S(1)} %get-tuple-element.129, s32[512]{0:T(512)S(1)} %bitcast.73), kind=kOutput, calls=%fused_computation.14.clone.1 | convolution fusion | flops 568328192 | bytes 1312768 | tf_op jit(solution)/shard_map/while/body/eval_jaxpr/tm,rt->mr/dot_general | solution.py:35
  823.7 31.9 %fusion.63 = bf16[1,1,512,128]{3,2,1,0:T(8,128)(2,1)S(1)} fusion(f32[512,128]{1,0:T(8,128)S(1)} %fusion.62, bf16[128,4096]{1,0:T(8,128)(2,1)S(1)} %copy-done.3, s32[512]{0:T(512)S(1)} %bitcast.74), kind=kOutput, calls=%fused_computation.23.clone.1 | convolution fusion | flops 568524800 | bytes 1443840 | tf_op jit(solution)/shard_map/while/body/eval_jaxpr/tm,rt->mr/dot_general | solution.py:35
  855.6 30.8 %fusion.60 = f32[512,128]{1,0:T(8,128)S(1)} fusion(bf16[128,4096]{1,0:T(8,128)(2,1)S(1)} %copy-done.3, s32[512]{0:T(512)S(1)} %bitcast.75), kind=kOutput, calls=%fused_computation.13.clone.1 | convolution fusion | flops 568328192 | bytes 1312768 | tf_op jit(solution)/shard_map/while/body/eval_jaxpr/tm,rt->mr/dot_general | solution.py:35
  886.5 31.3 %fusion.61 = bf16[1,1,512,128]{3,2,1,0:T(8,128)(2,1)S(1)} fusion(f32[512,128]{1,0:T(8,128)S(1)} %fusion.60, bf16[128,4096]{1,0:T(8,128)(2,1)S(1)} %get-tuple-element.129, s32[512]{0:T(512)S(1)} %bitcast.76), kind=kOutput, calls=%fused_computation.24.clone.1 | convolution fusion | flops 568524800 | bytes 1443840 | tf_op jit(solution)/shard_map/while/body/eval_jaxpr/tm,rt->mr/dot_general | solution.py:35
  918.3 30.8 %fusion.62 = f32[512,128]{1,0:T(8,128)S(1)} fusion(bf16[128,4096]{1,0:T(8,128)(2,1)S(1)} %get-tuple-element.129, s32[512]{0:T(512)S(1)} %bitcast.73), kind=kOutput, calls=%fused_computation.14.clone.1 | convolution fusion | flops 568328192 | bytes 1312768 | tf_op jit(solution)/shard_map/while/body/eval_jaxpr/tm,rt->mr/dot_general | solution.py:35
  949.2 31.9 %fusion.63 = bf16[1,1,512,128]{3,2,1,0:T(8,128)(2,1)S(1)} fusion(f32[512,128]{1,0:T(8,128)S(1)} %fusion.62, bf16[128,4096]{1,0:T(8,128)(2,1)S(1)} %copy-done.3, s32[512]{0:T(512)S(1)} %bitcast.74), kind=kOutput, calls=%fused_computation.23.clone.1 | convolution fusion | flops 568524800 | bytes 1443840 | tf_op jit(solution)/shard_map/while/body/eval_jaxpr/tm,rt->mr/dot_general | solution.py:35
  981.1 30.8 %fusion.60 = f32[512,128]{1,0:T(8,128)S(1)} fusion(bf16[128,4096]{1,0:T(8,128)(2,1)S(1)} %copy-done.3, s32[512]{0:T(512)S(1)} %bitcast.75), kind=kOutput, calls=%fused_computation.13.clone.1 | convolution fusion | flops 568328192 | bytes 1312768 | tf_op jit(solution)/shard_map/while/body/eval_jaxpr/tm,rt->mr/dot_general | solution.py:35
  1011.9 31.3 %fusion.61 = bf16[1,1,512,128]{3,2,1,0:T(8,128)(2,1)S(1)} fusion(f32[512,128]{1,0:T(8,128)S(1)} %fusion.60, bf16[128,4096]{1,0:T(8,128)(2,1)S(1)} %get-tuple-element.129, s32[512]{0:T(512)S(1)} %bitcast.76), kind=kOutput, calls=%fused_computation.24.clone.1 | convolution fusion | flops 568524800 | bytes 1443840 | tf_op jit(solution)/shard_map/while/body/eval_jaxpr/tm,rt->mr/dot_general | solution.py:35
  1047.8 18.1 %copy.22 = bf16[2,4096,128]{2,0,1:T(2,128)(2,1)} copy(bf16[2,4096,128]{2,1,0:T(8,128)(2,1)S(1)} %bitcast.70) | data formatting | bytes 4194304 | tf_op jit(solution)/shard_map/reshape | solution.py:44
  1065.9 9.3 all-to-all-start.1
  1075.2 1.9 copy.27
  1077.2 0.8 compare_select_fusion
  1077.9 0.7 gather_fusion
  1078.6 2.2 gather_fusion.1
  1080.8 0.1 copy.28
  1080.9 0.2 iota_compare_fusion.1
  1081.0 24.5 %all-to-all-done.1 = bf16[2,4096,128]{2,0,1:T(2,128)(2,1)S(1)} async-done(((bf16[2,4096,128]{2,0,1:T(2,128)(2,1)}), bf16[2,4096,128]{2,0,1:T(2,128)(2,1)S(1)}, u32[]{:S(2)}, u32[]{:S(2)}) %all-to-all-start.1) | async-done | bytes 2097184 | tf_op jit(solution)/shard_map/all_to_all | solution.py:48
  1105.6 1.3 copy-done.1
  1106.9 5.0 copy.23
  1111.9 6.1 reshape.86
  1118.0 20.5 %copy.24 = bf16[32,2,8,32,4,16]{0,5,4,3,2,1:T(8,128)(2,1)} copy(bf16[32,2,8,32,4,16]{3,4,5,2,0,1:T(4,128)(2,1)} %bitcast.64) | data formatting | bytes 4194304 | tf_op jit(solution)/shard_map/transpose | solution.py:49
  1138.5 8.5 bitcast_select_fusion
  1147.0 7.5 copy.25
  1154.5 6.3 fusion.41
  1160.8 0.1 copy.26
  1161.0 0.1 bitcast_reduce_fusion
  1161.1 0.6 convolution_bitcast_fusion
  1161.6 62.5 %all-reduce = f32[8,1024]{1,0:T(8,128)S(1)} all-reduce(f32[8,1024]{1,0:T(8,128)S(1)} %convolution_bitcast_fusion), channel_id=2, replica_groups=mesh['grp'=4,'wide'=32] {'grp','wide'}, use_global_device_ids=true, to_apply=%region_3.4.clone | all-reduce | flops 8192 | bytes 65536
  1224.1 0.7 dynamic-slice_multiply_fusion
  (43 shorter events, 0.5 us)
Async XLA Ops:
  0.6 1077.3 %copy-start = (s32[4096]{0:T(1024)S(1)}, s32[4096]{0:T(1024)}, u32[]{:S(2)}) copy-start(s32[4096]{0:T(1024)} %param.9) | copy-start | bytes 49156
  0.6 9.9 copy-start.5
  4.7 31.3 %all-to-all-start = ((bf16[2,8,64,1024]{3,1,0,2:T(8,128)(2,1)}), bf16[2,8,64,1024]{3,1,0,2:T(8,128)(2,1)S(1)}, u32[]{:S(2)}, u32[]{:S(2)}) async-start(bf16[2,8,64,1024]{3,1,0,2:T(8,128)(2,1)} %copy.18), calls=%async_computation | async-start | bytes 4194304 | tf_op jit(solution)/shard_map/all_to_all | solution.py:26
  36.2 3.4 copy-start.2
  40.1 30.9 %copy-start.3 = (bf16[128,4096]{1,0:T(8,128)(2,1)S(1)}, bf16[128,4096]{1,0:T(8,128)(2,1)}, u32[]{:S(2)}) copy-start(bf16[128,4096]{1,0:T(8,128)(2,1)} %get-tuple-element.130) | copy-start | bytes 3145732 | tf_op jit(solution)/shard_map/while
  165.6 30.9 %copy-start.3 = (bf16[128,4096]{1,0:T(8,128)(2,1)S(1)}, bf16[128,4096]{1,0:T(8,128)(2,1)}, u32[]{:S(2)}) copy-start(bf16[128,4096]{1,0:T(8,128)(2,1)} %get-tuple-element.130) | copy-start | bytes 3145732 | tf_op jit(solution)/shard_map/while
  291.0 30.9 %copy-start.3 = (bf16[128,4096]{1,0:T(8,128)(2,1)S(1)}, bf16[128,4096]{1,0:T(8,128)(2,1)}, u32[]{:S(2)}) copy-start(bf16[128,4096]{1,0:T(8,128)(2,1)} %get-tuple-element.130) | copy-start | bytes 3145732 | tf_op jit(solution)/shard_map/while
  416.5 30.9 %copy-start.3 = (bf16[128,4096]{1,0:T(8,128)(2,1)S(1)}, bf16[128,4096]{1,0:T(8,128)(2,1)}, u32[]{:S(2)}) copy-start(bf16[128,4096]{1,0:T(8,128)(2,1)} %get-tuple-element.130) | copy-start | bytes 3145732 | tf_op jit(solution)/shard_map/while
  541.9 30.9 %copy-start.3 = (bf16[128,4096]{1,0:T(8,128)(2,1)S(1)}, bf16[128,4096]{1,0:T(8,128)(2,1)}, u32[]{:S(2)}) copy-start(bf16[128,4096]{1,0:T(8,128)(2,1)} %get-tuple-element.130) | copy-start | bytes 3145732 | tf_op jit(solution)/shard_map/while
  667.4 30.9 %copy-start.3 = (bf16[128,4096]{1,0:T(8,128)(2,1)S(1)}, bf16[128,4096]{1,0:T(8,128)(2,1)}, u32[]{:S(2)}) copy-start(bf16[128,4096]{1,0:T(8,128)(2,1)} %get-tuple-element.130) | copy-start | bytes 3145732 | tf_op jit(solution)/shard_map/while
  792.8 30.9 %copy-start.3 = (bf16[128,4096]{1,0:T(8,128)(2,1)S(1)}, bf16[128,4096]{1,0:T(8,128)(2,1)}, u32[]{:S(2)}) copy-start(bf16[128,4096]{1,0:T(8,128)(2,1)} %get-tuple-element.130) | copy-start | bytes 3145732 | tf_op jit(solution)/shard_map/while
  918.3 30.9 %copy-start.3 = (bf16[128,4096]{1,0:T(8,128)(2,1)S(1)}, bf16[128,4096]{1,0:T(8,128)(2,1)}, u32[]{:S(2)}) copy-start(bf16[128,4096]{1,0:T(8,128)(2,1)} %get-tuple-element.130) | copy-start | bytes 3145732 | tf_op jit(solution)/shard_map/while
  1047.8 27.4 %copy-start.4 = (s32[4096,8]{0,1:T(8,128)S(1)}, s32[4096,8]{0,1:T(8,128)}, u32[]{:S(2)}) copy-start(s32[4096,8]{0,1:T(8,128)} %param.11) | copy-start | bytes 393220
  1065.9 39.6 %all-to-all-start.1 = ((bf16[2,4096,128]{2,0,1:T(2,128)(2,1)}), bf16[2,4096,128]{2,0,1:T(2,128)(2,1)S(1)}, u32[]{:S(2)}, u32[]{:S(2)}) async-start(bf16[2,4096,128]{2,0,1:T(2,128)(2,1)} %copy.22), calls=%async_computation.1 | async-start | bytes 4194304 | tf_op jit(solution)/shard_map/all_to_all | solution.py:48
  1105.6 1.3 copy-start.1
where the time goes:
time: 1230 us; the launch traced here: 1220 us
  matrix products  1010 us (82%)
  local copies, waits for them, and re-layouts  71.2 us (6%)
  blocking collectives  62.5 us (5%)
  waiting for transfers between devices  50 us (4%)
  starting transfers between devices  15.1 us (1%)
    dot_general x32, matrix products, product(): jnp.einsum('tm,rt->mr', table, values, preferred_element_type=jnp.float32)  999 us
    unnamed x1, blocking collectives  62.5 us
    all_to_all x1, waiting for transfers between devices, body(): lax.all_to_all(visibilities, 'grp', split_axis=2, concat_axis=3, tiled=True)  25.5 us
  transfers between devices with their start and end apart: 2, of which 2 were waited for; matrix products, arithmetic and copies ran while one was open for 0% of the time, Pallas kernels for 0%

commit v1 on v0

v1 whole, which is shorter than its diff:
```python
import math

import jax
import jax.numpy as jnp
import numpy as np
from jax import lax
from jax.experimental import pallas as pl
from jax.experimental.pallas import tpu as pltpu
from jax.sharding import Mesh
from jax.sharding import PartitionSpec as P

CH = 8
NB = 2048
NT = 4096
KL = 64
KB = 8
NBAND = 1024
NKB = 8

DEVS = 128
SLOTS = NT // DEVS
LANES = 128
N2 = NT // LANES
ALL = ("grp", "yx", "core")
F32 = jnp.float32
BF16 = jnp.bfloat16
NT_DIMS = (((1,), (1,)), ((), ()))


def inner_matrix():
    n = np.arange(LANES)
    angle = 2.0 * np.pi * ((n[:, None] * n[None, :]) % LANES) / LANES
    c, s = np.cos(angle) / math.sqrt(NT), np.sin(angle) / math.sqrt(NT)
    re = np.concatenate([c, s], axis=1)
    im = np.concatenate([-s, c], axis=1)
    return np.stack([re, im], axis=1).reshape(2 * LANES, 2 * LANES)


def twiddles():
    m2 = np.arange(N2)[:, None]
    t1 = np.arange(LANES)[None, :]
    angle = 2.0 * np.pi * ((m2 * t1) % NT) / NT
    return np.cos(angle).astype(np.float32), np.sin(angle).astype(np.float32)


def cmul_const(re, im, angle):
    c, s = math.cos(angle), math.sin(angle)
    return re * c + im * s, im * c - re * s


def dft4(x):
    (ar, ai), (br, bi), (cr, ci), (dr, di) = x
    pr, pi, qr, qi = ar + cr, ai + ci, ar - cr, ai - ci
    rr, ri, sr, si = br + dr, bi + di, br - dr, bi - di
    return [(pr + rr, pi + ri), (qr + si, qi - sr), (pr - rr, pi - ri), (qr - si, qi + sr)]


def dft8(x):
    even = dft4([x[0], x[2], x[4], x[6]])
    odd = dft4([x[1], x[3], x[5], x[7]])
    h = math.sqrt(0.5)
    o0 = odd[0]
    o1 = ((odd[1][0] + odd[1][1]) * h, (odd[1][1] - odd[1][0]) * h)
    o2 = (odd[2][1], -odd[2][0])
    o3 = ((odd[3][1] - odd[3][0]) * h, (odd[3][0] + odd[3][1]) * -h)
    lo, hi = [], []
    for (er, ei), (pr, pi) in zip(even, [o0, o1, o2, o3]):
        lo.append((er + pr, ei + pi))
        hi.append((er - pr, ei - pi))
    return lo + hi


def transform_kernel(rows_ref, x_ref, w_ref, twc_ref, tws_ref, o_ref, mid, d_ref, spec, picked):
    def outer(rg, carry):
        core = rg // 4
        r0 = pl.multiple_of((rg % 4) * 16, 16)
        for j in range(8):
            cols = slice(j * LANES, (j + 1) * LANES)
            x = [
                tuple(x_ref[2 * g + core, p, pl.ds(r0, 16), cols].astype(F32) for p in range(2))
                for g in range(4)
            ]
            for q, (re, im) in enumerate(dft4(x)):
                if j * q:
                    re, im = cmul_const(re, im, 2.0 * math.pi * j * q / N2)
                mid[q, j, 0] = re
                mid[q, j, 1] = im
        out0 = pl.multiple_of(rg * 16, 16)
        for q in range(4):
            for half in range(2):
                rows = slice(half * 8, half * 8 + 8)
                y = dft8([(mid[q, j, 0, rows], mid[q, j, 1, rows]) for j in range(8)])
                for p, (re, im) in enumerate(y):
                    m2 = q + 4 * p
                    c = twc_ref[m2 : m2 + 1, :]
                    s = tws_ref[m2 : m2 + 1, :]
                    mid[q, p, 0, rows] = re * c + im * s
                    mid[q, p, 1, rows] = im * c - re * s
            for p in range(8):
                for part in range(2):
                    d_ref[q + 4 * p, pl.ds(out0, 16), part * LANES : (part + 1) * LANES] = mid[
                        q, p, part
                    ].astype(BF16)
        return carry

    lax.fori_loop(0, 8, outer, 0)

    def inner(m2, carry):
        spec[pl.ds(pl.multiple_of(m2 * 256, 256), 256), :] = lax.dot_general(
            w_ref[...], d_ref[m2], NT_DIMS, preferred_element_type=F32
        )
        return carry

    lax.fori_loop(0, N2, inner, 0, unroll=2)

    def pick(step, carry):
        base = step * 32
        for u in range(32):
            row = pl.multiple_of(rows_ref[base + u], 2)
            picked[pl.ds(pl.multiple_of((base + u) * 2, 2), 2), :] = spec[pl.ds(row, 2), :]
        return carry

    lax.fori_loop(0, NT // 32, pick, 0)

    def narrow(step, carry):
        where = pl.ds(pl.multiple_of(step * 256, 256), 256)
        o_ref[where, :] = picked[where, :].astype(BF16)
        return carry

    lax.fori_loop(0, 2 * NT // 256, narrow, 0, unroll=2)


def mask_kernel(counts_ref, f_ref, o_ref):
    step = pl.program_id(0)
    column = lax.broadcasted_iota(jnp.int32, (KL, NB), 1)
    for s in range(8):
        rows = slice(s * KL, (s + 1) * KL)
        keep = column < counts_ref[step * 8 + s]
        o_ref[rows, :] = jnp.where(keep, f_ref[rows, :], jnp.zeros((), BF16))


def split3(x):
    a = x.astype(BF16)
    r = x - a.astype(F32)
    b = r.astype(BF16)
    return a, b, (r - b.astype(F32)).astype(BF16)


def iota(shape, axis):
    return lax.broadcasted_iota(jnp.int32, shape, axis)


def filter_kernel(x_ref, f_ref, col_ref, row_ref, kl_ref, band_ref, lhs, rhs):
    step = pl.program_id(0)
    r0 = pl.multiple_of(step * 16, 16)
    for k in range(16):
        lhs[:, k * LANES : (k + 1) * LANES] = x_ref[:, k, :, pl.ds(r0, 16), :].reshape(128, LANES)
    acc = lax.dot_general(lhs[...], f_ref[...], NT_DIMS, preferred_element_type=F32)
    own = ((iota((128, 512), 0) // 2) % 8) == (iota((128, 512), 1) // KL)
    acc = jnp.where(own, acc, 0.0)
    pairs = acc[:, 0:128] + acc[:, 128:256] + acc[:, 256:384] + acc[:, 384:512]
    mine = (pairs[:, :KL] + pairs[:, KL:]).astype(BF16)
    to, frm = iota((128, 128), 0), iota((128, 128), 1)
    order = jnp.where(frm == (to % 8) * 16 + to // 8, 1.0, 0.0).astype(BF16)
    kl_ref[...] = jnp.dot(order, mine, preferred_element_type=F32).astype(BF16)
    power = (acc * acc).reshape(8, 16, 512).sum(axis=1)
    spread = jnp.broadcast_to(power[:, None, :], (8, 8, 512)).reshape(64, 512)
    blocks = jnp.where(iota((64, 512), 1) // KB == iota((64, 512), 0), 1.0, 0.0).astype(BF16)
    table = sum(
        lax.dot_general(blocks, part, NT_DIMS, preferred_element_type=F32) for part in split3(spread)
    )
    band = col_ref[...]
    low = iota((64, 64), 1) % 8
    table = jnp.where((band[:, :64] % 8) == low, table, 0.0)
    rhs[pl.ds(pl.multiple_of(step * 64, 64), 64), :] = jnp.concatenate(
        [table, jnp.zeros((64, 64), F32)], axis=1
    )

    @pl.when(step == 3)
    def _():
        high = row_ref[0:1, :] // 8
        hot = jnp.where(iota((128, 256), 0) == high, 1.0, 0.0).astype(BF16)
        total = sum(jnp.dot(hot, part, preferred_element_type=F32) for part in split3(rhs[...]))
        band_ref[...] = total


def body(visibilities, filters, counts, m_of_slot, band_of_block):
    place = lax.axis_index(ALL)
    mine = lax.dynamic_slice_in_dim(m_of_slot, place * SLOTS, SLOTS)
    slot_counts = counts[mine]
    band = band_of_block[mine].reshape(SLOTS * NKB)
    band_col = jnp.broadcast_to(band[:, None], (SLOTS * NKB, 128))
    band_row = jnp.broadcast_to(band[None, :], (8, SLOTS * NKB))
    rows = (m_of_slot % N2) * (2 * LANES) + (m_of_slot // N2) * 2

    sent = visibilities.transpose(1, 0, 2, 3)
    local = lax.all_to_all(sent, ("grp", "core"), 0, 0, tiled=True)

    masked = pl.pallas_call(
        mask_kernel,
        out_shape=jax.ShapeDtypeStruct((SLOTS * KL, NB), BF16),
        grid_spec=pltpu.PrefetchScalarGridSpec(
            num_scalar_prefetch=1,
            grid=(4,),
            in_specs=[pl.BlockSpec((8 * KL, NB), lambda i, c: (i, 0))],
            out_specs=pl.BlockSpec((8 * KL, NB), lambda i, c: (i, 0)),
        ),
        name="mask",
    )(slot_counts, filters.reshape(SLOTS * KL, NB))

    tw_cos, tw_sin = twiddles()
    spectrum = pl.pallas_call(
        transform_kernel,
        out_shape=jax.ShapeDtypeStruct((2 * NT, LANES), BF16),
        grid_spec=pltpu.PrefetchScalarGridSpec(
            num_scalar_prefetch=1,
            grid=(1,),
            in_specs=[
                pl.BlockSpec((8, 2, 64, 1024), lambda i, r: (0, 0, 0, 0)),
                pl.BlockSpec((256, 256), lambda i, r: (0, 0)),
                pl.BlockSpec((N2, LANES), lambda i, r: (0, 0)),
                pl.BlockSpec((N2, LANES), lambda i, r: (0, 0)),
            ],
            out_specs=pl.BlockSpec((2 * NT, LANES), lambda i, r: (0, 0)),
            scratch_shapes=[
                pltpu.VMEM((4, 8, 2, 16, LANES), F32),
                pltpu.VMEM((N2, LANES, 2 * LANES), BF16),
                pltpu.VMEM((2 * NT, LANES), F32),
                pltpu.VMEM((2 * NT, LANES), F32),
            ],
        ),
        name="transform",
    )(rows, local, jnp.asarray(inner_matrix(), BF16), jnp.asarray(tw_cos), jnp.asarray(tw_sin))

    moved = lax.all_to_all(spectrum.reshape(DEVS, 2 * SLOTS, LANES), ALL, 0, 0, tiled=True)

    kl, part = pl.pallas_call(
        filter_kernel,
        out_shape=(
            jax.ShapeDtypeStruct((SLOTS * 2 * CH, KL), BF16),
            jax.ShapeDtypeStruct((DEVS, 128), F32),
        ),
        grid=(4,),
        in_specs=[
            pl.BlockSpec((4, 16, 2, 2 * SLOTS, LANES), lambda i: (0, 0, 0, 0, 0)),
            pl.BlockSpec((8 * KL, NB), lambda i: (i, 0)),
            pl.BlockSpec((64, 128), lambda i: (i, 0)),
            pl.BlockSpec((8, 256), lambda i: (0, 0)),
        ],
        out_specs=(
            pl.BlockSpec((128, KL), lambda i: (i, 0)),
            pl.BlockSpec((DEVS, 128), lambda i: (0, 0)),
        ),
        scratch_shapes=[pltpu.VMEM((128, NB), BF16), pltpu.VMEM((256, 128), F32)],
        name="filter",
    )(moved.reshape(4, 16, 2, 2 * SLOTS, LANES), masked, band_col, band_row)

    shares = lax.all_to_all(part[:, None, :], ALL, 0, 0, tiled=True)
    power = shares.reshape(DEVS, 128).sum(axis=0)[:64].reshape(CH, 8)
    return kl.reshape(SLOTS, 2, CH, KL), power * (NBAND / (NT * KL))


def solution(mesh):
    fine = Mesh(mesh.devices.reshape(4, 16, 2), ALL)
    wide = ("yx", "core")
    placed = (P(None, None, wide, "grp"), P(ALL, None, None), P(), P(), P())
    return jax.shard_map(
        body,
        mesh=fine,
        in_specs=placed,
        out_specs=(P(ALL, None, None, None), P(None, ALL)),
        check_vma=False,
    )
```

time: 1230 us -> 116 us (0.09)
  matrix products: 1010 us -> 0 us
  local copies, waits for them, and re-layouts: 71.2 us -> 12 us
  blocking collectives: 62.5 us -> 14.3 us
  Pallas kernels: 0 us -> 30 us
    dot_general x34 -> x0, matrix products: 1010 us -> none  [the longest x32 999 us: product(): jnp.einsum('tm,rt->mr', table, values, preferred_element_type=jnp.float32)]
    unnamed x1 -> x0, blocking collectives: 62.5 us -> none
    pallas_call x0 -> x3, Pallas kernels: none -> 30 us  [the longest x1 13.8 us: body(): pl.pallas_call(transform_kernel, out_shape=jax.ShapeDtypeStruct((2 * NT,...]
    reshape x3 -> x0, local copies, waits for them, and re-layouts: 24.2 us -> none  [the longest x1 18.1 us: body(): spectrum = blocks.transpose(1, 0, 2, 3).reshape(2, NT, rows)]
    transpose x1 -> x0, local copies, waits for them, and re-layouts: 20.5 us -> none  [body(): moved.reshape(2, slots, groups, wides, channels, base_dev)]
    all_to_all x0 -> x1, blocking collectives: none -> 14.3 us  [body(): shares = lax.all_to_all(part[:, None, :], ALL, 0, 0, tiled=True)]
  transfers between devices with their start and end apart: 2 -> 2, of which waited for: 2 -> 2; matrix products, arithmetic and copies ran while one was open for 0% -> 5% of each run, Pallas kernels for 0% -> 7%
where the time goes in v1:
time: 116 us
  waiting for transfers between devices  42.7 us (37%)
  Pallas kernels  30 us (26%)
  starting transfers between devices  15 us (13%)
  blocking collectives  14.3 us (12%)
  local copies, waits for them, and re-layouts  12 us (10%)
    all_to_all x1, waiting for transfers between devices, body(): local = lax.all_to_all(sent, ('grp', 'core'), 0, 0, tiled=True)  25.6 us
    all_to_all x1, waiting for transfers between devices, body(): lax.all_to_all(spectrum.reshape(DEVS, 2 * SLOTS, LANES), ALL, 0, 0, tiled...  17.1 us
    all_to_all x1, blocking collectives, body(): shares = lax.all_to_all(part[:, None, :], ALL, 0, 0, tiled=True)  14.3 us
    pallas_call x1, Pallas kernels, body(): pl.pallas_call(transform_kernel, out_shape=jax.ShapeDtypeStruct((2 * NT,...  13.8 us
    pallas_call x1, Pallas kernels, body(): pl.pallas_call(filter_kernel, out_shape=(jax.ShapeDtypeStruct((SLOTS * 2...  8.43 us
    all_to_all x1, starting transfers between devices, body(): lax.all_to_all(spectrum.reshape(DEVS, 2 * SLOTS, LANES), ALL, 0, 0, tiled...  8.09 us
    pallas_call x1, Pallas kernels, body(): pl.pallas_call(mask_kernel, out_shape=jax.ShapeDtypeStruct((SLOTS * KL, N...  7.8 us
    all_to_all x1, starting transfers between devices, body(): local = lax.all_to_all(sent, ('grp', 'core'), 0, 0, tiled=True)  6.93 us
  transfers between devices with their start and end apart: 2, of which 2 were waited for; matrix products, arithmetic and copies ran while one was open for 5% of the time, Pallas kernels for 7%

profile of v1, /device:TPU:1, one launch (start us, length us, event | category | flops | bytes accessed | tf_op | source)
XLA Modules:
  0.0 115.7 jit_solution(635530746271621376)
XLA Ops:
  0.6 0.0 copy-start
  0.6 3.2 %copy.18 = bf16[2,8,64,1024]{3,2,0,1:T(8,128)(2,1)} copy(bf16[2,8,64,1024]{3,2,1,0:T(8,128)(2,1)} %param.8) | data formatting | bytes 4194304 | tf_op args[0]
  3.8 0.0 copy-start.4
  3.8 6.9 %all-to-all-start = ((bf16[8,2,64,1024]{3,2,1,0:T(8,128)(2,1)}), bf16[8,2,64,1024]{3,2,1,0:T(8,128)(2,1)S(1)}, u32[]{:S(2)}, u32[]{:S(2)}) async-start(bf16[8,2,64,1024]{3,2,1,0:T(8,128)(2,1)} %bitcast.12), calls=%async_computation | async-start | bytes 4194304 | tf_op jit(solution)/shard_map/all_to_all | solution.py:197
  10.8 0.0 copy-done.4
  10.8 0.6 fusion.1.rows_ref
  11.4 25.6 %all-to-all-done.x_ref = bf16[8,2,64,1024]{3,2,1,0:T(8,128)(2,1)S(1)} async-done(((bf16[8,2,64,1024]{3,2,1,0:T(8,128)(2,1)}), bf16[8,2,64,1024]{3,2,1,0:T(8,128)(2,1)S(1)}, u32[]{:S(2)}, u32[]{:S(2)}) %all-to-all-start) | async-done | bytes 2097184 | tf_op jit(solution)/shard_map/all_to_all | solution.py:197
  37.0 0.0 copy-start.1
  37.0 1.3 %copy-done.1 = bf16[8,2,64,1024]{3,2,1,0:T(8,128)(2,1)} copy-done((bf16[8,2,64,1024]{3,2,1,0:T(8,128)(2,1)}, bf16[8,2,64,1024]{3,2,1,0:T(8,128)(2,1)S(1)}, u32[]{:S(2)}) %copy-start.1) | copy-done | bytes 2097176
  38.3 13.8 %transform.1 = bf16[8192,128]{1,0:T(8,128)(2,1)} custom-call(s32[4096]{0:T(1024)} %fusion.1.rows_ref, bf16[8,2,64,1024]{3,2,1,0:T(8,128)(2,1)} %copy-done.1, bf16[256,256]{1,0:T(8,128)(2,1)} %constant.62.clone.w_ref, f32[32,128]{1,0:T(8,128)} %constant.63.clone.twc_ref, f32[32,128]{1,0:T(8,128)} %constant.64.clone.tws_ref), custom_call_target="tpu_custom_call" | custom-call | tf_op jit(solution)/shard_map/transform/pallas_call | solution.py:212
  52.1 0.0 copy-start.3
  52.1 8.1 %all-to-all-start.1 = ((bf16[128,64,128]{2,1,0:T(8,128)(2,1)}), bf16[128,64,128]{2,1,0:T(8,128)(2,1)S(1)}, u32[]{:S(2)}, u32[]{:S(2)}) async-start(bf16[128,64,128]{2,1,0:T(8,128)(2,1)} %bitcast.11), calls=%async_computation.1 | async-start | bytes 4194304 | tf_op jit(solution)/shard_map/all_to_all | solution.py:235
  60.2 0.0 copy-done.3
  60.2 2.0 %copy.15 = s32[4096,8]{1,0:T(8,128)} copy(s32[4096,8]{0,1:T(8,128)S(1)} %copy-done.3) | data formatting | bytes 262144 | tf_op args[4]
  62.2 0.1 compare_select_fusion
  62.3 0.0 copy-done
  62.3 1.2 %gather_fusion = s32[32]{0:T(128)} fusion(s32[4096]{0:T(1024)S(1)} %copy-done, s32[1024]{0:T(1024)S(1)} %pad_clamp_fusion), kind=kCustom, calls=%fused_computation | custom fusion | bytes 384 | tf_op jit(solution)/shard_map/gather | solution.py:190
  63.5 2.2 %gather_fusion.1 = s32[32,8]{1,0:T(8,128)S(1)} fusion(s32[4096,8]{1,0:T(8,128)} %copy.15, s32[1024]{0:T(1024)S(1)} %pad_clamp_fusion), kind=kCustom, calls=%fused_computation.1 | custom fusion | bytes 2176 | tf_op jit(solution)/shard_map/gather | solution.py:191
  65.6 0.1 broadcast_in_dim.20
  65.7 7.8 %mask.1.f_ref = bf16[2048,2048]{1,0:T(8,128)(2,1)} custom-call(s32[32]{0:T(128)} %gather_fusion, bf16[2048,2048]{1,0:T(8,128)(2,1)} %bitcast.10), custom_call_target="tpu_custom_call" | custom-call | tf_op jit(solution)/shard_map/mask/pallas_call | solution.py:199
  73.5 17.1 %all-to-all-done.1 = bf16[128,64,128]{2,1,0:T(8,128)(2,1)S(1)} async-done(((bf16[128,64,128]{2,1,0:T(8,128)(2,1)}), bf16[128,64,128]{2,1,0:T(8,128)(2,1)S(1)}, u32[]{:S(2)}, u32[]{:S(2)}) %all-to-all-start.1) | async-done | bytes 2097184 | tf_op jit(solution)/shard_map/all_to_all | solution.py:235
  90.7 0.0 copy-start.2
  90.7 0.6 broadcast_in_dim.22.row_ref
  91.3 0.8 broadcast_in_dim.21.col_ref
  92.1 0.0 copy-done.2
  92.1 8.4 %filter.1 = (bf16[512,64]{1,0:T(8,128)(2,1)}, f32[128,128]{1,0:T(8,128)}) custom-call(bf16[4,16,2,64,128]{4,3,2,1,0:T(8,128)(2,1)} %bitcast.13, bf16[2048,2048]{1,0:T(8,128)(2,1)} %mask.1.f_ref, s32[256,128]{1,0:T(8,128)} %broadcast_in_dim.21.col_ref, s32[8,256]{1,0:T(8,128)} %broadcast_in_dim.22.row_ref), custom_call_target="tpu_custom_call" | custom-call | tf_op jit(solution)/shard_map/filter/pallas_call | solution.py:237
  100.5 14.3 %all_to_all.15 = f32[128,1,128]{2,1,0:T(1,128)S(1)} all-to-all(f32[128,1,128]{2,1,0:T(1,128)} %bitcast.14), channel_id=1, replica_groups=mesh['grp'=4,'yx'=16,'core'=2] {'grp','yx','core'}, dimensions={0} | all-to-all | bytes 131072 | tf_op jit(solution)/shard_map/all_to_all | solution.py:258
  114.8 0.2 reduce_sum.9
  115.0 0.7 mul.39
  (2 shorter events, 0.0 us)
Async XLA Ops:
  0.6 61.6 %copy-start = (s32[4096]{0:T(1024)S(1)}, s32[4096]{0:T(1024)}, u32[]{:S(2)}) copy-start(s32[4096]{0:T(1024)} %param.10) | copy-start | bytes 49156
  3.8 6.9 %copy-start.4 = (s32[4096]{0:T(1024)S(1)}, s32[4096]{0:T(1024)}, u32[]{:S(2)}) copy-start(s32[4096]{0:T(1024)} %param.11) | copy-start | bytes 49156
  3.8 33.1 %all-to-all-start = ((bf16[8,2,64,1024]{3,2,1,0:T(8,128)(2,1)}), bf16[8,2,64,1024]{3,2,1,0:T(8,128)(2,1)S(1)}, u32[]{:S(2)}, u32[]{:S(2)}) async-start(bf16[8,2,64,1024]{3,2,1,0:T(8,128)(2,1)} %bitcast.12), calls=%async_computation | async-start | bytes 4194304 | tf_op jit(solution)/shard_map/all_to_all | solution.py:197
  37.0 1.3 %copy-start.1 = (bf16[8,2,64,1024]{3,2,1,0:T(8,128)(2,1)}, bf16[8,2,64,1024]{3,2,1,0:T(8,128)(2,1)S(1)}, u32[]{:S(2)}) copy-start(bf16[8,2,64,1024]{3,2,1,0:T(8,128)(2,1)S(1)} %all-to-all-done.x_ref) | copy-start | bytes 6291460
  52.1 8.1 %copy-start.3 = (s32[4096,8]{0,1:T(8,128)S(1)}, s32[4096,8]{0,1:T(8,128)}, u32[]{:S(2)}) copy-start(s32[4096,8]{0,1:T(8,128)} %param.12) | copy-start | bytes 393220
  52.1 38.6 %all-to-all-start.1 = ((bf16[128,64,128]{2,1,0:T(8,128)(2,1)}), bf16[128,64,128]{2,1,0:T(8,128)(2,1)S(1)}, u32[]{:S(2)}, u32[]{:S(2)}) async-start(bf16[128,64,128]{2,1,0:T(8,128)(2,1)} %bitcast.11), calls=%async_computation.1 | async-start | bytes 4194304 | tf_op jit(solution)/shard_map/all_to_all | solution.py:235
  90.7 1.4 %copy-start.2 = (bf16[128,64,128]{2,1,0:T(8,128)(2,1)}, bf16[128,64,128]{2,1,0:T(8,128)(2,1)S(1)}, u32[]{:S(2)}) copy-start(bf16[128,64,128]{2,1,0:T(8,128)(2,1)S(1)} %all-to-all-done.1) | copy-start | bytes 6291460
